TPU v7x, 32 devices: a whole 2x2x4 slice. The times are simulated.
32 devices in a mesh: harm: 8 (over y, x, core), mode: 4 (over z).
Axes of the slice: x: 2, y: 2, z: 4, core: 2. Of those that a mesh axis runs over, the one named last changes fastest.
Arguments:
- mode_vectors: float32 [49152, 1024], P('harm', 'mode'), may hold values from -0.09375 to 0.09375
- weights: float32 [49152, 1024], P('harm', 'mode'), may hold values from -0.1875 to 0.1875
- cotangent: float32 [49152, 1024], P('harm', 'mode'), may hold values from -6 to 6
- eigenvalues: float32 [1024], replicated, may hold values from 0 to 4
- eigen_cotangent: float32 [1024], replicated, may hold values from -6 to 6
- slab_rows: int32 [4096], replicated, may hold values from 0 to 49151, as said below
Outputs:
- slab: float32 [4096, 49152], P('mode', 'harm')
Inputs may be any that keep to these rules, and one draw needn't show every extreme that they name: `slab_rows`: each block of 6144 consecutive harmonics (0 to 6143, 6144 to 12287 and so on) holds exactly 512 of the slab rows.
All inputs are finite; a program needn't handle non-finite values.
Results may differ from a plain program's by a relative error of at most 0.0001.
Values sent between devices are 32-bit elements; how exact they have to be, the bound alone decides.
A program may use at most 128 MiB of HBM per device.

v0:
```python
import jax
import jax.numpy as jnp
from jax import lax
from jax.sharding import PartitionSpec as P

regular = 0.01
precision = lax.Precision.HIGHEST


def product(left, right, left_dim, right_dim):
    return lax.dot_general(
        left,
        right,
        (((left_dim,), (right_dim,)), ((), ())),
        precision=precision,
        preferred_element_type=jnp.float32,
    )


def weigh_gap(block, row_ids, col_ids, eigenvalues, eigen_cotangent):
    eigen_rows = lax.dynamic_slice_in_dim(eigenvalues, row_ids, block.shape[0])
    eigen_cols = lax.dynamic_slice_in_dim(eigenvalues, col_ids, block.shape[1])
    slope_cols = lax.dynamic_slice_in_dim(eigen_cotangent, col_ids, block.shape[1])
    differ = eigen_cols[None, :] - eigen_rows[:, None]
    factor = differ / (differ * differ + regular)
    rows = row_ids + lax.broadcasted_iota(jnp.int32, block.shape, 0)
    cols = col_ids + lax.broadcasted_iota(jnp.int32, block.shape, 1)
    return factor * block + jnp.where(rows == cols, slope_cols[None, :], 0.0)


def pick_rows(table, slab_rows, harm_index):
    row_count = table.shape[0]
    offset = slab_rows - harm_index * row_count
    inside = (offset >= 0) & (offset < row_count)
    picked = jnp.take(table, jnp.clip(offset, 0, row_count - 1), axis=0)
    return jnp.where(inside[:, None], picked, 0.0)


def gather_weights(weights, slab_rows, harm_index, harm_count, mode_count):
    width = weights.shape[1]
    with jax.named_scope("pick"):
        picked = pick_rows(weights, slab_rows, harm_index)
    piece = slab_rows.shape[0] // (harm_count * mode_count)
    picked = picked.reshape(mode_count, harm_count, piece, width)
    with jax.named_scope("sum_weights"):
        picked = lax.psum_scatter(picked, "harm", scatter_dimension=1, tiled=True)
    picked = picked.reshape(mode_count, piece, width)
    with jax.named_scope("swap"):
        swapped = lax.all_to_all(picked, "mode", split_axis=0, concat_axis=2, tiled=True)
    with jax.named_scope("spread_weights"):
        return lax.all_gather(
            swapped.reshape(piece, mode_count * width), "harm", axis=0, tiled=True
        )


def plain(
    mode_vectors,
    weights,
    cotangent,
    eigenvalues,
    eigen_cotangent,
    slab_rows,
    harm_count,
    mode_count,
):
    harm_index = lax.axis_index("harm")
    width = mode_vectors.shape[1]
    modes = width * mode_count
    full = lax.all_gather(mode_vectors, "mode", axis=1, tiled=True)
    owned_weights = gather_weights(weights, slab_rows, harm_index, harm_count, mode_count)
    gram = product(full, cotangent, 0, 0)
    gram = lax.psum_scatter(gram, "harm", scatter_dimension=0, tiled=True)
    weighted = weigh_gap(
        gram,
        harm_index * (modes // harm_count),
        lax.axis_index("mode") * width,
        eigenvalues,
        eigen_cotangent,
    )
    weighted = lax.all_gather(weighted, "mode", axis=1, tiled=True)
    weighted = lax.all_gather(weighted, "harm", axis=0, tiled=True)
    return product(product(owned_weights, weighted, 1, 0), full, 1, 1)


def solution(mesh):
    harm_count = mesh.shape["harm"]
    mode_count = mesh.shape["mode"]
    placed = (P("harm", "mode"), P("harm", "mode"), P("harm", "mode"), P(), P(), P())

    def local(*operands):
        return plain(*operands, harm_count, mode_count)

    return jax.shard_map(
        local, mesh=mesh, in_specs=placed, out_specs=P("mode", "harm"), check_vma=False
    )
```

profile of v0, /device:TPU:0, one launch (start us, length us, event | category | flops | bytes accessed | tf_op | source)
XLA Modules:
  0.0 702.6 jit_solution(5876162007898497041)
XLA Ops:
  7.4 0.0 copy-start
  7.4 0.0 all-gather.6.cloned.1.call-start
  7.4 0.7 all-gather.6.cloned.1.call-update
  8.1 0.0 reduce-scatter.3.cloned.1.call-start
  8.1 0.0 copy-done
  8.2 18.9 %gather_fusion = f32[4096,256]{1,0:T(8,128)} fusion(f32[6144,256]{1,0:T(8,128)} %param.7, s32[4096]{0:T(1024)S(1)} %fusion.3), kind=kCustom, calls=%fused_computation | custom fusion | bytes 8404992 | tf_op jit(solution)/shard_map/pick/jit(_take)/gather | solution.py:35
  27.2 5.6 copy.10
  32.7 5.5 select_select_fusion
  38.3 0.0 reduce-scatter.3.cloned.1.call-update
  38.3 0.0 reduce-scatter.5.cloned.1.call-start
  38.3 399.3 %all-gather.6.cloned.1.call-done = f32[6144,1024]{1,0:T(8,128)} async-done(((f32[6144,256]{1,0:T(8,128)}), f32[6144,1024]{1,0:T(8,128)}) %all-gather.6.cloned.1.call-update) | async-done | bytes 25165840 | tf_op jit(solution)/shard_map/all_gather | solution.py:69
  437.7 44.0 %fusion.4 = f32[1024,256]{1,0:T(8,128)} fusion(f32[6144,1024]{1,0:T(8,128)} %all-gather.6.cloned.1.call-done, f32[6144,256]{1,0:T(8,128)} %param.8), kind=kOutput, calls=%fused_computation.13 | convolution fusion | flops 19327352832 | bytes 32505856 | tf_op jit(solution)/shard_map/dot_general | solution.py:11
  481.6 0.0 reduce-scatter.5.cloned.1.call-update
  481.6 0.0 all-gather.4.cloned.1.call-start
  481.7 0.0 reduce-scatter.3.cloned.1.call-done
  481.7 19.2 %all_to_all.15 = f32[4,128,256]{1,2,0:T(8,128)} all-to-all(f32[4,128,256]{1,2,0:T(8,128)} %bitcast.19), channel_id=1, replica_groups=mesh['harm'=8,'mode'=4] {'mode'}, dimensions={0} | all-to-all | bytes 1048576 | tf_op jit(solution)/shard_map/swap/all_to_all | solution.py:49
  500.9 0.0 all-gather.4.cloned.1.call-update
  500.9 0.0 all-gather.8.cloned.1.call-start
  501.0 0.8 dynamic_slice.10
  501.7 0.8 dynamic_slice.9
  502.5 0.8 dynamic_slice.11
  503.2 12.6 %reduce-scatter.5.cloned.1.call-done = f32[128,256]{1,0:T(8,128)} async-done(((f32[1024,256]{1,0:T(8,128)}), f32[128,256]{1,0:T(8,128)}) %reduce-scatter.5.cloned.1.call-update) | async-done | bytes 131088 | tf_op jit(solution)/shard_map/reduce_scatter | solution.py:72
  515.8 1.0 fusion.2
  516.9 15.9 %all_gather.14 = f32[128,1024]{1,0:T(8,128)} all-gather(f32[128,256]{1,0:T(8,128)S(1)} %fusion.2), channel_id=1, replica_groups=mesh['harm'=8,'mode'=4] {'mode'}, dimensions={1}, use_global_device_ids=true | all-gather | bytes 655360 | tf_op jit(solution)/shard_map/all_gather | solution.py:80
  532.8 0.0 all-gather.8.cloned.1.call-update
  532.8 22.0 %all-gather.4.cloned.1.call-done = f32[1024,1024]{0,1:T(8,128)} async-done(((f32[128,1024]{0,1:T(8,128)}), f32[1024,1024]{0,1:T(8,128)}) %all-gather.4.cloned.1.call-update) | async-done | bytes 4194320 | tf_op jit(solution)/shard_map/spread_weights/all_gather | solution.py:51
  554.8 38.4 %all-gather.8.cloned.1.call-done = f32[1024,1024]{1,0:T(8,128)} async-done(((f32[128,1024]{1,0:T(8,128)}), f32[1024,1024]{1,0:T(8,128)}) %all-gather.8.cloned.1.call-update) | async-done | bytes 4194320 | tf_op jit(solution)/shard_map/all_gather | solution.py:81
  593.2 16.6 %fusion.5 = f32[1024,1024]{1,0:T(8,128)S(1)} fusion(f32[1024,1024]{0,1:T(8,128)} %all-gather.4.cloned.1.call-done, f32[1024,1024]{1,0:T(8,128)} %all-gather.8.cloned.1.call-done), kind=kOutput, calls=%fused_computation.14 | convolution fusion | flops 12884901888 | bytes 12582912 | tf_op jit(solution)/shard_map/dot_general | solution.py:11
  609.8 85.2 %fusion.6 = f32[1024,6144]{1,0:T(8,128)} fusion(f32[1024,1024]{1,0:T(8,128)S(1)} %fusion.5, f32[6144,1024]{1,0:T(8,128)} %all-gather.6.cloned.1.call-done), kind=kOutput, calls=%fused_computation.15 | convolution fusion | flops 77309411328 | bytes 54525952 | tf_op jit(solution)/shard_map/dot_general | solution.py:11
  (6 shorter events, 0.1 us)
Async XLA Ops:
  7.4 0.8 copy-start
  7.4 430.3 %all-gather.6.cloned.1.call-start = ((), (), s32[]{:S(2)}) async-start(), calls=%async_computation.5 | async-start | bytes 31457280 | tf_op jit(solution)/shard_map/all_gather | solution.py:69
  8.1 473.6 %reduce-scatter.3.cloned.1.call-start = ((), (), s32[]{:S(2)}) async-start(), calls=%async_computation.3 | async-start | bytes 4718592 | tf_op jit(solution)/shard_map/sum_weights/reduce_scatter | solution.py:46
  38.3 477.6 %reduce-scatter.5.cloned.1.call-start = ((), (), s32[]{:S(2)}) async-start(), calls=%async_computation.6 | async-start | bytes 1179648 | tf_op jit(solution)/shard_map/reduce_scatter | solution.py:72
  481.6 73.2 %all-gather.4.cloned.1.call-start = ((), (), s32[]{:S(2)}) async-start(), calls=%async_computation.4 | async-start | bytes 4718592 | tf_op jit(solution)/shard_map/spread_weights/all_gather | solution.py:51
  500.9 92.3 %all-gather.8.cloned.1.call-start = ((), (), s32[]{:S(2)}) async-start(), calls=%async_computation.7 | async-start | bytes 4718592 | tf_op jit(solution)/shard_map/all_gather | solution.py:81
Sparse Core Ops, SparseCore 0:
  9.7 427.8 all-gather.5
Sparse Core Ops, SparseCore 1:
  38.4 53.7 reduce-scatter.2
  481.7 34.1 reduce-scatter.4
  517.6 37.2 all-gather.3
  556.8 36.4 all-gather.7
where the time goes:
time: 703 us
  waiting for transfers between devices  473 us (67%)
  matrix products  146 us (21%)
  blocking collectives  35.1 us (5%)
  local copies, waits for them, and re-layouts  26.8 us (4%)
  between operations  15.1 us (2%)
    all_gather x1, waiting for transfers between devices, plain(): full = lax.all_gather(mode_vectors, 'mode', axis=1, tiled=True)  399 us
    dot_general x3, matrix products, product(): lax.dot_general(left, right, (((left_dim,), (right_dim,)), ((), ())), pre...  146 us
    all_gather x1, waiting for transfers between devices, plain(): weighted = lax.all_gather(weighted, 'harm', axis=0, tiled=True)  38.4 us
    gather x2, local copies, waits for them, and re-layouts, pick_rows(): picked = jnp.take(table, jnp.clip(offset, 0, row_count - 1), axis=0)  24.5 us
    all_gather x1, waiting for transfers between devices, gather_weights(): lax.all_gather(swapped.reshape(piece, mode_count * width), 'harm', axis=0...  22 us
    all_to_all x1, blocking collectives, gather_weights(): lax.all_to_all(picked, 'mode', split_axis=0, concat_axis=2, tiled=True)  19.2 us
    all_gather x1, blocking collectives, plain(): weighted = lax.all_gather(weighted, 'mode', axis=1, tiled=True)  15.9 us
  transfers between devices with their start and end apart: 5, of which 4 were waited for; matrix products, arithmetic and copies ran while one was open for 11% of the time, Pallas kernels for 0%

commit v1 on v0

--- a/solution.py
+++ b/solution.py
@@ -46,7 +46,12 @@
         picked = lax.psum_scatter(picked, "harm", scatter_dimension=1, tiled=True)
     picked = picked.reshape(mode_count, piece, width)
     with jax.named_scope("swap"):
-        swapped = lax.all_to_all(picked, "mode", split_axis=0, concat_axis=2, tiled=True)
+        swapped = jnp.concatenate(
+            lax.all_to_all(
+                jnp.stack(jnp.split(picked, lax.axis_size("mode"), 0), axis=0), "mode", 0, 0
+            ),
+            2,
+        )
     with jax.named_scope("spread_weights"):
         return lax.all_gather(
             swapped.reshape(piece, mode_count * width), "harm", axis=0, tiled=True

time: 703 us -> 703 us (level)
  no operation moved by 1% of the time
where the time goes in v1:
time: 703 us
  waiting for transfers between devices  472 us (67%)
  matrix products  146 us (21%)
  blocking collectives  34.2 us (5%)
  local copies, waits for them, and re-layouts  29.1 us (4%)
  between operations  15.1 us (2%)
    all_gather x1, waiting for transfers between devices, plain(): full = lax.all_gather(mode_vectors, 'mode', axis=1, tiled=True)  399 us
    dot_general x3, matrix products, product(): lax.dot_general(left, right, (((left_dim,), (right_dim,)), ((), ())), pre...  146 us
    all_gather x1, waiting for transfers between devices, plain(): weighted = lax.all_gather(weighted, 'harm', axis=0, tiled=True)  38.4 us
    gather x2, local copies, waits for them, and re-layouts, pick_rows(): picked = jnp.take(table, jnp.clip(offset, 0, row_count - 1), axis=0)  24.5 us
    all_gather x1, waiting for transfers between devices, gather_weights(): lax.all_gather(swapped.reshape(piece, mode_count * width), 'harm', axis=0...  22 us
    all_to_all x1, blocking collectives, gather_weights(): lax.all_to_all(jnp.stack(jnp.split(picked, lax.axis_size('mode'), 0), axi...  18.2 us
    all_gather x1, blocking collectives, plain(): weighted = lax.all_gather(weighted, 'mode', axis=1, tiled=True)  16 us
  transfers between devices with their start and end apart: 5, of which 4 were waited for; matrix products, arithmetic and copies ran while one was open for 11% of the time, Pallas kernels for 0%

profile of v1, /device:TPU:0, one launch (start us, length us, event | category | flops | bytes accessed | tf_op | source)
XLA Modules:
  0.0 702.7 jit_solution(4570062755073579900)
XLA Ops:
  7.4 0.0 copy-start
  7.4 0.0 all-gather.6.cloned.1.call-start
  7.4 0.7 all-gather.6.cloned.1.call-update
  8.1 0.0 all-reduce.3.cloned.1.call-start
  8.1 0.0 copy-done
  8.2 18.9 %gather_fusion = f32[4096,256]{1,0:T(8,128)} fusion(f32[6144,256]{1,0:T(8,128)} %param.7, s32[4096]{0:T(1024)S(1)} %fusion.3), kind=kCustom, calls=%fused_computation | custom fusion | bytes 8404992 | tf_op jit(solution)/shard_map/pick/jit(_take)/gather | solution.py:35
  27.1 5.6 copy.13
  32.7 5.5 select_select_fusion
  38.2 0.0 all-reduce.3.cloned.1.call-update
  38.2 0.0 copy-start.1
  38.2 0.0 reduce-scatter.5.cloned.1.call-start
  38.3 399.4 %all-gather.6.cloned.1.call-done = f32[6144,1024]{1,0:T(8,128)} async-done(((f32[6144,256]{1,0:T(8,128)}), f32[6144,1024]{1,0:T(8,128)}) %all-gather.6.cloned.1.call-update) | async-done | bytes 25165840 | tf_op jit(solution)/shard_map/all_gather | solution.py:74
  437.7 44.0 %fusion.4 = f32[1024,256]{1,0:T(8,128)} fusion(f32[6144,1024]{1,0:T(8,128)} %all-gather.6.cloned.1.call-done, f32[6144,256]{1,0:T(8,128)} %param.8), kind=kOutput, calls=%fused_computation.14 | convolution fusion | flops 19327352832 | bytes 32505856 | tf_op jit(solution)/shard_map/dot_general | solution.py:11
  481.6 0.0 reduce-scatter.5.cloned.1.call-update
  481.7 0.0 all-gather.4.cloned.1.call-start
  481.7 0.0 copy-done.1
  481.7 0.6 dynamic-slice
  482.3 0.0 all-reduce.3.cloned.1.call-done
  482.3 1.7 constant_dynamic-slice_fusion
  484.1 18.2 %all_to_all.5 = f32[4,1,128,256]{2,3,1,0:T(8,128)} all-to-all(f32[4,1,128,256]{2,3,1,0:T(8,128)S(1)} %constant_dynamic-slice_fusion), channel_id=1, replica_groups=mesh['harm'=8,'mode'=4] {'mode'}, dimensions={0} | all-to-all | bytes 1048576 | tf_op jit(solution)/shard_map/swap/all_to_all | solution.py:50
  502.3 0.0 all-gather.4.cloned.1.call-update
  502.3 0.0 all-gather.8.cloned.1.call-start
  502.3 0.8 dynamic_slice.10
  503.1 0.8 dynamic_slice.9
  503.9 0.8 dynamic_slice.11
  504.6 11.2 %reduce-scatter.5.cloned.1.call-done = f32[128,256]{1,0:T(8,128)} async-done(((f32[1024,256]{1,0:T(8,128)}), f32[128,256]{1,0:T(8,128)}) %reduce-scatter.5.cloned.1.call-update) | async-done | bytes 131088 | tf_op jit(solution)/shard_map/reduce_scatter | solution.py:77
  515.9 1.0 fusion.2
  516.9 16.0 %all_gather.14 = f32[128,1024]{1,0:T(8,128)} all-gather(f32[128,256]{1,0:T(8,128)S(1)} %fusion.2), channel_id=1, replica_groups=mesh['harm'=8,'mode'=4] {'mode'}, dimensions={1}, use_global_device_ids=true | all-gather | bytes 655360 | tf_op jit(solution)/shard_map/all_gather | solution.py:85
  532.9 0.0 all-gather.8.cloned.1.call-update
  532.9 22.0 %all-gather.4.cloned.1.call-done = f32[1024,1024]{0,1:T(8,128)} async-done(((f32[128,1024]{0,1:T(8,128)}), f32[1024,1024]{0,1:T(8,128)}) %all-gather.4.cloned.1.call-update) | async-done | bytes 4194320 | tf_op jit(solution)/shard_map/spread_weights/all_gather | solution.py:56
  554.8 38.4 %all-gather.8.cloned.1.call-done = f32[1024,1024]{1,0:T(8,128)} async-done(((f32[128,1024]{1,0:T(8,128)}), f32[1024,1024]{1,0:T(8,128)}) %all-gather.8.cloned.1.call-update) | async-done | bytes 4194320 | tf_op jit(solution)/shard_map/all_gather | solution.py:86
  593.3 16.6 %fusion.5 = f32[1024,1024]{1,0:T(8,128)S(1)} fusion(f32[1024,1024]{0,1:T(8,128)} %all-gather.4.cloned.1.call-done, f32[1024,1024]{1,0:T(8,128)} %all-gather.8.cloned.1.call-done), kind=kOutput, calls=%fused_computation.15 | convolution fusion | flops 12884901888 | bytes 12582912 | tf_op jit(solution)/shard_map/dot_general | solution.py:11
  609.8 85.2 %fusion.6 = f32[1024,6144]{1,0:T(8,128)} fusion(f32[1024,1024]{1,0:T(8,128)S(1)} %fusion.5, f32[6144,1024]{1,0:T(8,128)} %all-gather.6.cloned.1.call-done), kind=kOutput, calls=%fused_computation.16 | convolution fusion | flops 77309411328 | bytes 54525952 | tf_op jit(solution)/shard_map/dot_general | solution.py:11
  (4 shorter events, 0.0 us)
Async XLA Ops:
  7.4 0.8 copy-start
  7.4 430.3 %all-gather.6.cloned.1.call-start = ((), (), s32[]{:S(2)}) async-start(), calls=%async_computation.3 | async-start | bytes 31457280 | tf_op jit(solution)/shard_map/all_gather | solution.py:74
  8.1 474.2 %all-reduce.3.cloned.1.call-start = ((), (), s32[]{:S(2)}) async-start(), calls=%async_computation.6 | async-start | bytes 8388608
  38.2 443.5 %copy-start.1 = (u32[32]{0:T(128)S(1)}, u32[32]{0:T(128)}, u32[]{:S(2)}) copy-start(u32[32]{0:T(128)} %constant.42) | copy-start | bytes 388
  38.2 477.6 %reduce-scatter.5.cloned.1.call-start = ((), (), s32[]{:S(2)}) async-start(), calls=%async_computation.4 | async-start | bytes 1179648 | tf_op jit(solution)/shard_map/reduce_scatter | solution.py:77
  481.7 73.2 %all-gather.4.cloned.1.call-start = ((), (), s32[]{:S(2)}) async-start(), calls=%async_computation.2 | async-start | bytes 4718592 | tf_op jit(solution)/shard_map/spread_weights/all_gather | solution.py:56
  502.3 91.0 %all-gather.8.cloned.1.call-start = ((), (), s32[]{:S(2)}) async-start(), calls=%async_computation.5 | async-start | bytes 4718592 | tf_op jit(solution)/shard_map/all_gather | solution.py:86
Sparse Core Ops, SparseCore 0:
  9.7 427.8 all-gather.5
Sparse Core Ops, SparseCore 1:
  38.3 83.1 all-reduce.2
  481.7 34.1 reduce-scatter.4
  517.6 37.2 all-gather.3
  556.8 36.4 all-gather.7
